TPU v7x, 512 devices: a whole 4x8x8 slice. The times are simulated.
512 devices in a mesh: blk: 32 (over x_lo, y, core), tm: 16 (over z, x_hi).
Axes of the slice: x: 4 (x_hi: 2, x_lo: 2; x = x_hi * 2 + x_lo), y: 8, z: 8, core: 2. Of those that a mesh axis runs over, the one named last changes fastest.
Arguments:
- clips: bfloat16 [32, 32, 16, 36, 256], P('blk', 'tm'), may hold values from -6 to 6
- cotangent: bfloat16 [32, 32, 16, 36, 256], P('blk', 'tm'), may hold values from -6 to 6
- conv_master: float32 [3072, 256], P('blk'), may hold values from -0.125 to 0.125
- first_moment: float32 [3072, 256], P('blk'), may hold values from -3 to 3
- second_moment: float32 [3072, 256], P('blk'), may hold values from 0.1 to 100
- norm_gain: float32 [256], replicated, may hold values from 0.5 to 1.5
- norm_bias: float32 [256], replicated, may hold values from -3 to 3
Outputs:
- block_out: bfloat16 [32, 32, 16, 36, 256], P('blk', 'tm')
- input_grad: bfloat16 [32, 32, 16, 36, 256], P('blk', 'tm')
- new_master: float32 [3072, 256], P('blk')
- new_first: float32 [3072, 256], P('blk')
- new_second: float32 [3072, 256], P('blk')
- norm_grads: float32 [2, 256], replicated
All inputs are finite; a program needn't handle non-finite values.
Results may differ from a plain program's by a relative error of at most 0.0063.
Values may be sent and summed in bfloat16 or wider, within the bound.
A program may use at most 64 MiB of HBM per device.

v0:
```python
import jax
import jax.numpy as jnp
from jax import lax
from jax.sharding import PartitionSpec as P

GROUPS = 32
beta_one = 0.9
beta_two = 0.999
learn_rate = 0.003
adam_eps = 1e-08
bias_first = 1.0 - 0.9**10
bias_second = 1.0 - 0.999**10


def extended(block, sides, width):
    for axis, dim in sides:
        count = lax.axis_size(axis)
        forward = [(i, i + 1) for i in range(count - 1)]
        backward = [(target, source) for source, target in forward]
        low = lax.ppermute(
            lax.slice_in_dim(block, block.shape[dim] - width, None, axis=dim), axis, forward
        )
        high = lax.ppermute(lax.slice_in_dim(block, 0, width, axis=dim), axis, backward)
        block = jnp.concatenate([low, block, high], axis=dim)
    return block


def norm_act(field, gain, bias):
    shape = field.shape
    grouped = field.reshape(shape[:-3] + (shape[-3] * shape[-2], GROUPS, shape[-1] // GROUPS))
    center = jnp.mean(grouped, axis=(-3, -1), keepdims=True)
    spread = jnp.mean((grouped - center) ** 2, axis=(-3, -1), keepdims=True)
    normed = ((grouped - center) * lax.rsqrt(spread + 1e-05)).reshape(shape)
    return jax.nn.silu(normed * gain + bias)


def adam_update(gradient, master, first, second):
    new_first = beta_one * first + (1.0 - beta_one) * gradient
    new_second = beta_two * second + (1.0 - beta_two) * gradient * gradient
    update = new_first / bias_first / (jnp.sqrt(new_second / bias_second) + adam_eps)
    return (master - learn_rate * update, new_first, new_second)


def shards(clips, cotangent, conv_master, first_moment, second_moment, norm_gain, norm_bias):
    f32 = jnp.float32
    frames, height, width, channels = (
        clips.shape[1],
        clips.shape[2],
        clips.shape[3],
        clips.shape[4],
    )
    weights = lax.all_gather(conv_master.astype(jnp.bfloat16), "blk", axis=0, tiled=True)
    inputs32 = clips.astype(f32)
    act32, pullback = jax.vjp(norm_act, inputs32, norm_gain, norm_bias)
    act = act32.astype(jnp.bfloat16)
    act_padded = jnp.pad(act, ((0, 0), (0, 0), (1, 1), (1, 1), (0, 0)))
    space32 = jnp.zeros(clips.shape, f32)
    for row_tap in range(3):
        for col_tap in range(3):
            tap_index = 3 * row_tap + col_tap
            window = act_padded[:, :, row_tap : row_tap + height, col_tap : col_tap + width, :]
            tap = weights[tap_index * channels : (tap_index + 1) * channels]
            space32 = space32 + jnp.einsum(
                "bfhwc,cd->bfhwd", window, tap, preferred_element_type=f32
            )
    space = space32.astype(jnp.bfloat16)
    space_padded = extended(space, (("tm", 1),), 1)
    temporal = jnp.zeros(clips.shape, f32)
    for frame_tap in range(3):
        tap = weights[(9 + frame_tap) * channels : (10 + frame_tap) * channels]
        temporal = temporal + jnp.einsum(
            "bfhwc,cd->bfhwd",
            space_padded[:, frame_tap : frame_tap + frames],
            tap,
            preferred_element_type=f32,
        )
    block_out = (inputs32 + temporal).astype(jnp.bfloat16)
    back_weights = lax.all_gather(conv_master.astype(jnp.bfloat16), "blk", axis=0, tiled=True)
    grad_padded = extended(cotangent, (("tm", 1),), 1)
    space_grad32 = jnp.zeros(clips.shape, f32)
    temporal_grads = []
    for frame_tap in range(3):
        tap = back_weights[(9 + frame_tap) * channels : (10 + frame_tap) * channels]
        space_grad32 = space_grad32 + jnp.einsum(
            "bfhwd,cd->bfhwc",
            grad_padded[:, 2 - frame_tap : 2 - frame_tap + frames],
            tap,
            preferred_element_type=f32,
        )
        temporal_grads.append(
            jnp.einsum(
                "bfhwc,bfhwd->cd",
                space_padded[:, frame_tap : frame_tap + frames],
                cotangent,
                preferred_element_type=f32,
            )
        )
    space_grad = space_grad32.astype(jnp.bfloat16)
    sgrad_padded = jnp.pad(space_grad, ((0, 0), (0, 0), (1, 1), (1, 1), (0, 0)))
    act_grad = jnp.zeros(clips.shape, f32)
    spatial_grads = []
    for row_tap in range(3):
        for col_tap in range(3):
            tap_index = 3 * row_tap + col_tap
            tap = back_weights[tap_index * channels : (tap_index + 1) * channels]
            window = act_padded[:, :, row_tap : row_tap + height, col_tap : col_tap + width, :]
            spatial_grads.append(
                jnp.einsum("bfhwc,bfhwd->cd", window, space_grad, preferred_element_type=f32)
            )
            back_window = sgrad_padded[
                :, :, 2 - row_tap : 2 - row_tap + height, 2 - col_tap : 2 - col_tap + width, :
            ]
            act_grad = act_grad + jnp.einsum(
                "bfhwd,cd->bfhwc", back_window, tap, preferred_element_type=f32
            )
    input_term, gain_grad, bias_grad = pullback(act_grad)
    input_grad = (cotangent.astype(f32) + input_term).astype(jnp.bfloat16)
    local_gradient = jnp.concatenate(spatial_grads + temporal_grads, axis=0)
    norm_grads = lax.psum(jnp.stack([gain_grad, bias_grad]), ("blk", "tm"))
    row_block = lax.psum_scatter(local_gradient, "blk", scatter_dimension=0, tiled=True)
    gradient = lax.psum(row_block, "tm")
    new_master, new_first, new_second = adam_update(
        gradient, conv_master, first_moment, second_moment
    )
    return (block_out, input_grad, new_master, new_first, new_second, norm_grads)


def solution(mesh):
    placed = (
        P("blk", "tm", None, None, None),
        P("blk", "tm", None, None, None),
        P("blk", None),
        P("blk", None),
        P("blk", None),
        P(),
        P(),
    )
    return jax.shard_map(
        shards,
        mesh=mesh,
        in_specs=placed,
        out_specs=(
            P("blk", "tm", None, None, None),
            P("blk", "tm", None, None, None),
            P("blk", None),
            P("blk", None),
            P("blk", None),
            P(),
        ),
        check_vma=False,
    )
```

profile of v0, /device:TPU:8, one launch (start us, length us, event | category | flops | bytes accessed | tf_op | source)
XLA Modules:
  0.0 426.8 jit_solution(4757618439813596500)
XLA Ops:
  7.2 1.5 convert_element_type.38
  8.8 1.3 copy.26
  10.9 4.9 %collective-permute-start.3 = (bf16[1,1,16,36,256]{4,3,2,1,0:T(8,128)(2,1)S(1)}, bf16[1,1,16,36,256]{4,3,2,1,0:T(8,128)(2,1)S(1)}, u32[]{:S(2)}, u32[]{:S(2)}) collective-permute-start(bf16[1,1,16,36,256]{4,3,2,1,0:T(8,128)(2,1)S(1)} %get-tuple-element.25), channel_id=1, source_target_pairs={{0,1},{1,2},{2,3},{3,4},{4,5},{5,6},{6,7},{7,8},{8,9},{9,10},{10,1... | collective-permute-start | bytes 884744 | tf_op jit(solution)/shard_map/ppermute | solution.py:20
  15.8 1.3 collective-permute-start.2
  18.3 11.4 %collective-permute-done.3 = bf16[1,1,16,36,256]{4,3,2,1,0:T(8,128)(2,1)S(1)} collective-permute-done((bf16[1,1,16,36,256]{4,3,2,1,0:T(8,128)(2,1)S(1)}, bf16[1,1,16,36,256]{4,3,2,1,0:T(8,128)(2,1)S(1)}, u32[]{:S(2)}, u32[]{:S(2)}) %collective-permute-start.3) | collective-permute-done | bytes 294944 | tf_op jit(solution)/shard_map/ppermute | solution.py:20
  30.5 50.4 %all-gather.2.cloned.1.call-done = bf16[3072,256]{1,0:T(8,128)(2,1)} async-done(((bf16[96,256]{1,0:T(8,128)(2,1)}), bf16[3072,256]{1,0:T(8,128)(2,1)}) %all-gather.2.cloned.1.call-update) | async-done | bytes 1572880 | tf_op jit(solution)/shard_map/all_gather | solution.py:52
  80.9 1.5 fusion.51
  82.9 1.4 fusion.9
  87.8 1.2 fusion.26
  91.7 3.0 fusion.14
  94.7 1.1 fusion.49
  95.8 1.1 fusion.48
  96.9 1.1 fusion.47
  98.0 1.1 fusion.46
  99.1 1.1 fusion.45
  100.2 1.1 fusion.44
  101.3 1.1 fusion.43
  106.0 5.0 %collective-permute-start = (bf16[1,1,16,36,256]{4,3,2,1,0:T(8,128)(2,1)S(1)}, bf16[1,1,16,36,256]{4,3,2,1,0:T(8,128)(2,1)S(1)}, u32[]{:S(2)}, u32[]{:S(2)}) collective-permute-start(bf16[1,1,16,36,256]{4,3,2,1,0:T(8,128)(2,1)S(1)} %get-tuple-element.26), channel_id=1, source_target_pairs={{0,1},{1,2},{2,3},{3,4},{4,5},{5,6},{6,7},{7,8},{8,9},{9,10},{10,1... | collective-permute-start | bytes 884744 | tf_op jit(solution)/shard_map/ppermute | solution.py:20
  111.0 1.1 fusion.42
  112.1 1.4 collective-permute-start.1
  113.5 1.1 fusion.41
  114.6 10.7 %collective-permute-done = bf16[1,1,16,36,256]{4,3,2,1,0:T(8,128)(2,1)S(1)} collective-permute-done((bf16[1,1,16,36,256]{4,3,2,1,0:T(8,128)(2,1)S(1)}, bf16[1,1,16,36,256]{4,3,2,1,0:T(8,128)(2,1)S(1)}, u32[]{:S(2)}, u32[]{:S(2)}) %collective-permute-start) | collective-permute-done | bytes 294944 | tf_op jit(solution)/shard_map/ppermute | solution.py:20
  125.3 1.2 fusion.40
  126.5 1.1 fusion.39
  128.4 1.2 fusion.38
  131.7 98.4 %psum.15 = f32[2,256]{1,0:T(2,128)} all-reduce(f32[2,256]{1,0:T(2,128)S(1)} %pad_maximum_fusion.4), channel_id=1, replica_groups=mesh['blk'=32,'tm'=16] {'blk','tm'}, use_global_device_ids=true, to_apply=%region_14.15 | all-reduce | flops 512 | bytes 4096 | tf_op jit(solution)/shard_map/psum | solution.py:119
  230.1 1.4 fusion.129
  231.6 1.4 fusion.127
  233.0 19.1 %reduce-scatter.2.cloned.1.call-done = f32[96,256]{1,0:T(8,128)} async-done(((f32[3072,256]{1,0:T(8,128)}), f32[96,256]{1,0:T(8,128)}) %reduce-scatter.2.cloned.1.call-update) | async-done | bytes 98320 | tf_op jit(solution)/shard_map/reduce_scatter | solution.py:120
  252.1 2.2 fusion.11
  255.3 163.4 %all-reduce.4.cloned.1.call-done = f32[96,256]{1,0:T(8,128)} async-done(((f32[96,256]{1,0:T(8,128)}), f32[96,256]{1,0:T(8,128)}) %all-reduce.4.cloned.1.call-update) | async-done | bytes 98320 | tf_op jit(solution)/shard_map/psum | solution.py:121
  418.7 1.6 multiply_subtract_fusion
  (91 shorter events, 16.6 us)
Async XLA Ops:
  7.2 73.8 %all-gather.2.cloned.1.call-start = ((), (), s32[]{:S(2)}) async-start(), calls=%async_computation.1 | async-start | bytes 1622016 | tf_op jit(solution)/shard_map/all_gather | solution.py:52
  8.7 8.4 %copy-start = (bf16[1,2,16,36,256]{4,2,3,1,0:T(8,128)(2,1)S(1)}, bf16[1,2,16,36,256]{4,2,3,1,0:T(8,128)(2,1)}, u32[]{:S(2)}) copy-start(bf16[1,2,16,36,256]{4,2,3,1,0:T(8,128)(2,1)} %param.7) | copy-start | bytes 1769476
  8.8 243.3 %reduce-scatter.2.cloned.1.call-start = ((), (), s32[]{:S(2)}) async-start(), calls=%async_computation.2 | async-start | bytes 3244032 | tf_op jit(solution)/shard_map/reduce_scatter | solution.py:120
  10.9 18.9 %collective-permute-start.3 = (bf16[1,1,16,36,256]{4,3,2,1,0:T(8,128)(2,1)S(1)}, bf16[1,1,16,36,256]{4,3,2,1,0:T(8,128)(2,1)S(1)}, u32[]{:S(2)}, u32[]{:S(2)}) collective-permute-start(bf16[1,1,16,36,256]{4,3,2,1,0:T(8,128)(2,1)S(1)} %get-tuple-element.25), channel_id=1, source_target_pairs={{0,1},{1,2},{2,3},{3,4},{4,5},{5,6},{6,7},{7,8},{8,9},{9,10},{10,1... | collective-permute-start | bytes 884744 | tf_op jit(solution)/shard_map/ppermute | solution.py:20
  15.8 67.1 %collective-permute-start.2 = (bf16[1,1,16,36,256]{4,3,2,1,0:T(8,128)(2,1)}, bf16[1,1,16,36,256]{4,3,2,1,0:T(8,128)(2,1)}, u32[]{:S(2)}, u32[]{:S(2)}) collective-permute-start(bf16[1,1,16,36,256]{4,3,2,1,0:T(8,128)(2,1)} %get-tuple-element.24), channel_id=1, source_target_pairs={{1,0},{2,1},{3,2},{4,3},{5,4},{6,5},{7,6},{8,7},{9,8},{10,9},{11,1... | collective-permute-start | bytes 884744 | tf_op jit(solution)/shard_map/ppermute | solution.py:23
  17.9 64.5 %copy-start.2 = (bf16[1,2,16,36,256]{4,2,3,1,0:T(8,128)(2,1)S(1)}, bf16[1,2,16,36,256]{4,2,3,1,0:T(8,128)(2,1)}, u32[]{:S(2)}) copy-start(bf16[1,2,16,36,256]{4,2,3,1,0:T(8,128)(2,1)} %param.8) | copy-start | bytes 1769476
  29.8 0.7 copy-start.12
  80.9 1.6 copy-start.1
  87.1 0.7 copy-start.15
  87.1 0.7 copy-start.16
  89.0 1.1 copy-start.5
  90.1 1.7 copy-start.3
  106.0 19.3 %collective-permute-start = (bf16[1,1,16,36,256]{4,3,2,1,0:T(8,128)(2,1)S(1)}, bf16[1,1,16,36,256]{4,3,2,1,0:T(8,128)(2,1)S(1)}, u32[]{:S(2)}, u32[]{:S(2)}) collective-permute-start(bf16[1,1,16,36,256]{4,3,2,1,0:T(8,128)(2,1)S(1)} %get-tuple-element.26), channel_id=1, source_target_pairs={{0,1},{1,2},{2,3},{3,4},{4,5},{5,6},{6,7},{7,8},{8,9},{9,10},{10,1... | collective-permute-start | bytes 884744 | tf_op jit(solution)/shard_map/ppermute | solution.py:20
  112.1 13.3 %copy-start.4 = (bf16[1,2,16,36,256]{4,2,3,1,0:T(8,128)(2,1)S(1)}, bf16[1,2,16,36,256]{4,2,3,1,0:T(8,128)(2,1)}, u32[]{:S(2)}) copy-start(bf16[1,2,16,36,256]{4,2,3,1,0:T(8,128)(2,1)} %param.8) | copy-start | bytes 1769476
  112.1 15.6 %collective-permute-start.1 = (bf16[1,1,16,36,256]{4,3,2,1,0:T(8,128)(2,1)S(1)}, bf16[1,1,16,36,256]{4,3,2,1,0:T(8,128)(2,1)S(1)}, u32[]{:S(2)}, u32[]{:S(2)}) collective-permute-start(bf16[1,1,16,36,256]{4,3,2,1,0:T(8,128)(2,1)S(1)} %get-tuple-element.27), channel_id=1, source_target_pairs={{1,0},{2,1},{3,2},{4,3},{5,4},{6,5},{7,6},{8,7},{9,8},{10,9},{11,1... | collective-permute-start | bytes 884744 | tf_op jit(solution)/shard_map/ppermute | solution.py:23
  125.3 1.2 copy-start.8
  127.7 0.7 copy-start.10
  129.7 1.1 copy-start.6
  129.7 289.0 %all-reduce.4.cloned.1.call-start = ((), (), s32[]{:S(2)}) async-start(), calls=%async_computation.3 | async-start | bytes 196608 | tf_op jit(solution)/shard_map/psum | solution.py:121
  131.7 99.9 %copy-start.11 = (bf16[1,1,16,36,256]{4,3,2,1,0:T(8,128)(2,1)S(1)}, bf16[1,1,16,36,256]{4,3,2,1,0:T(8,128)(2,1)}, u32[]{:S(2)}) copy-start(bf16[1,1,16,36,256]{4,3,2,1,0:T(8,128)(2,1)} %copy-done.10) | copy-start | bytes 884740
  231.6 20.5 %copy-start.9 = (bf16[1,1,16,36,256]{4,3,2,1,0:T(8,128)(2,1)S(1)}, bf16[1,1,16,36,256]{4,3,2,1,0:T(8,128)(2,1)}, u32[]{:S(2)}) copy-start(bf16[1,1,16,36,256]{4,3,2,1,0:T(8,128)(2,1)} %copy-done.8) | copy-start | bytes 884740
  254.3 164.3 %copy-start.7 = (f32[96,256]{1,0:T(8,128)S(1)}, f32[96,256]{1,0:T(8,128)}, u32[]{:S(2)}) copy-start(f32[96,256]{1,0:T(8,128)} %param.9) | copy-start | bytes 294916
  254.3 164.3 %copy-start.13 = (f32[96,256]{1,0:T(8,128)S(1)}, f32[96,256]{1,0:T(8,128)}, u32[]{:S(2)}) copy-start(f32[96,256]{1,0:T(8,128)} %param.10) | copy-start | bytes 294916
  254.4 164.3 %copy-start.14 = (f32[96,256]{1,0:T(8,128)S(1)}, f32[96,256]{1,0:T(8,128)}, u32[]{:S(2)}) copy-start(f32[96,256]{1,0:T(8,128)} %param.11) | copy-start | bytes 294916
Sparse Core Ops, SparseCore 0:
  10.7 70.1 all-gather.1
  129.8 122.2 reduce-scatter.1
  255.0 163.6 all-reduce.3
where the time goes:
time: 427 us
  waiting for transfers between devices  255 us (60%)
  blocking collectives  98.4 us (23%)
  matrix products  29.6 us (7%)
  between operations  14.1 us (3%)
  starting transfers between devices  12.7 us (3%)
  local copies, waits for them, and re-layouts  9.06 us (2%)
  other arithmetic  7.8 us (2%)
    psum x1, waiting for transfers between devices, shards(): gradient = lax.psum(row_block, 'tm')  163 us
    psum x1, blocking collectives, shards(): norm_grads = lax.psum(jnp.stack([gain_grad, bias_grad]), ('blk', 'tm'))  98.4 us
    all_gather x1, waiting for transfers between devices, shards(): lax.all_gather(conv_master.astype(jnp.bfloat16), 'blk', axis=0, tiled=True)  50.4 us
    ppermute x2, waiting for transfers between devices, extended(): lax.ppermute(lax.slice_in_dim(block, block.shape[dim] - width, None, axis...  22.2 us
    reduce_scatter x1, waiting for transfers between devices, shards(): lax.psum_scatter(local_gradient, 'blk', scatter_dimension=0, tiled=True)  19.1 us
    ppermute x2, starting transfers between devices, extended(): lax.ppermute(lax.slice_in_dim(block, block.shape[dim] - width, None, axis...  9.9 us
    dot_general x9, matrix products, shards(): jnp.einsum('bfhwc,bfhwd->cd', window, space_grad, preferred_element_type=...  9.86 us
  transfers between devices with their start and end apart: 7, of which 5 were waited for; matrix products, arithmetic and copies ran while one was open for 4% of the time, Pallas kernels for 0%

commit v1 on v0

--- a/solution.py
+++ b/solution.py
@@ -118,7 +118,7 @@
     local_gradient = jnp.concatenate(spatial_grads + temporal_grads, axis=0)
     norm_grads = lax.psum(jnp.stack([gain_grad, bias_grad]), ("blk", "tm"))
     row_block = lax.psum_scatter(local_gradient, "blk", scatter_dimension=0, tiled=True)
-    gradient = lax.psum(row_block, "tm")
+    gradient = jnp.sum(lax.all_gather(row_block, "tm"), axis=0)
     new_master, new_first, new_second = adam_update(
         gradient, conv_master, first_moment, second_moment
     )

time: 427 us -> 372 us (0.87)
  the two profiles are of different devices: /device:TPU:8 before, /device:TPU:1 now
where the time goes in v1:
time: 372 us
  waiting for transfers between devices  197 us (53%)
  blocking collectives  105 us (28%)
  matrix products  25.8 us (7%)
  between operations  14.1 us (4%)
  starting transfers between devices  12.6 us (3%)
  local copies, waits for them, and re-layouts  8.65 us (2%)
  other arithmetic  8.42 us (2%)
    reduce_scatter x1, waiting for transfers between devices, shards(): lax.psum_scatter(local_gradient, 'blk', scatter_dimension=0, tiled=True)  124 us
    psum x1, blocking collectives, shards(): norm_grads = lax.psum(jnp.stack([gain_grad, bias_grad]), ('blk', 'tm'))  105 us
    all_gather x1, waiting for transfers between devices, shards(): lax.all_gather(conv_master.astype(jnp.bfloat16), 'blk', axis=0, tiled=True)  61.3 us
    ppermute x2, waiting for transfers between devices, extended(): lax.ppermute(lax.slice_in_dim(block, block.shape[dim] - width, None, axis...  12.1 us
    dot_general x9, matrix products, shards(): jnp.einsum('bfhwc,bfhwd->cd', window, space_grad, preferred_element_type=...  9.87 us
    ppermute x2, starting transfers between devices, extended(): lax.ppermute(lax.slice_in_dim(block, block.shape[dim] - width, None, axis...  9.8 us
  transfers between devices with their start and end apart: 7, of which 4 were waited for; matrix products, arithmetic and copies ran while one was open for 3% of the time, Pallas kernels for 0%

profile of v1, /device:TPU:1, one launch (start us, length us, event | category | flops | bytes accessed | tf_op | source)
XLA Modules:
  0.0 371.6 jit_solution(16759843771920146645)
XLA Ops:
  7.2 1.5 convert_element_type.38
  8.8 1.3 copy.26
  10.1 0.8 fusion.179
  10.9 5.5 %collective-permute-start.3 = (bf16[1,1,16,36,256]{4,3,2,1,0:T(8,128)(2,1)S(1)}, bf16[1,1,16,36,256]{4,3,2,1,0:T(8,128)(2,1)S(1)}, u32[]{:S(2)}, u32[]{:S(2)}) collective-permute-start(bf16[1,1,16,36,256]{4,3,2,1,0:T(8,128)(2,1)S(1)} %get-tuple-element.25), channel_id=1, source_target_pairs={{0,1},{1,2},{2,3},{3,4},{4,5},{5,6},{6,7},{7,8},{8,9},{9,10},{10,1... | collective-permute-start | bytes 884744 | tf_op jit(solution)/shard_map/ppermute | solution.py:20
  16.4 1.3 collective-permute-start.2
  18.9 2.1 collective-permute-done.3
  21.7 61.3 %all-gather.4.cloned.1.call-done = bf16[3072,256]{1,0:T(8,128)(2,1)} async-done(((bf16[96,256]{1,0:T(8,128)(2,1)}), bf16[3072,256]{1,0:T(8,128)(2,1)}) %all-gather.4.cloned.1.call-update) | async-done | bytes 1572880 | tf_op jit(solution)/shard_map/all_gather | solution.py:52
  83.1 1.5 fusion.51
  85.1 1.3 fusion.9
  89.9 1.2 fusion.26
  91.1 1.1 copy-done.5
  93.9 3.0 fusion.14
  96.9 1.1 fusion.49
  98.0 1.1 fusion.48
  99.0 1.1 fusion.47
  100.1 1.1 fusion.46
  101.2 1.1 fusion.45
  102.3 1.1 fusion.44
  103.4 1.1 fusion.43
  108.1 4.3 %collective-permute-start = (bf16[1,1,16,36,256]{4,3,2,1,0:T(8,128)(2,1)S(1)}, bf16[1,1,16,36,256]{4,3,2,1,0:T(8,128)(2,1)S(1)}, u32[]{:S(2)}, u32[]{:S(2)}) collective-permute-start(bf16[1,1,16,36,256]{4,3,2,1,0:T(8,128)(2,1)S(1)} %get-tuple-element.26), channel_id=1, source_target_pairs={{0,1},{1,2},{2,3},{3,4},{4,5},{5,6},{6,7},{7,8},{8,9},{9,10},{10,1... | collective-permute-start | bytes 884744 | tf_op jit(solution)/shard_map/ppermute | solution.py:20
  112.5 1.1 fusion.42
  113.6 1.4 collective-permute-start.1
  115.0 1.1 fusion.41
  116.1 10.0 %collective-permute-done = bf16[1,1,16,36,256]{4,3,2,1,0:T(8,128)(2,1)S(1)} collective-permute-done((bf16[1,1,16,36,256]{4,3,2,1,0:T(8,128)(2,1)S(1)}, bf16[1,1,16,36,256]{4,3,2,1,0:T(8,128)(2,1)S(1)}, u32[]{:S(2)}, u32[]{:S(2)}) %collective-permute-start) | collective-permute-done | bytes 294944 | tf_op jit(solution)/shard_map/ppermute | solution.py:20
  126.1 1.2 fusion.40
  127.3 1.1 fusion.39
  129.2 1.2 fusion.38
  130.5 123.5 %reduce-scatter.2.cloned.1.call-done = f32[96,256]{1,0:T(8,128)} async-done(((f32[3072,256]{1,0:T(8,128)}), f32[96,256]{1,0:T(8,128)}) %reduce-scatter.2.cloned.1.call-update) | async-done | bytes 98320 | tf_op jit(solution)/shard_map/reduce_scatter | solution.py:120
  254.1 0.9 copy.36
  255.0 104.9 %psum.7 = f32[2,256]{1,0:T(2,128)} all-reduce(f32[2,256]{1,0:T(2,128)S(1)} %pad_maximum_fusion.4), channel_id=1, replica_groups=mesh['blk'=32,'tm'=16] {'blk','tm'}, use_global_device_ids=true, to_apply=%region_14.15 | all-reduce | flops 512 | bytes 4096 | tf_op jit(solution)/shard_map/psum | solution.py:119
  361.9 0.9 copy.35
  362.8 1.5 reduce_sum.138
  (92 shorter events, 14.6 us)
Async XLA Ops:
  7.2 75.9 %all-gather.4.cloned.1.call-start = ((), (), s32[]{:S(2)}) async-start(), calls=%async_computation.1 | async-start | bytes 1622016 | tf_op jit(solution)/shard_map/all_gather | solution.py:52
  8.7 8.9 %copy-start = (bf16[1,2,16,36,256]{4,2,3,1,0:T(8,128)(2,1)S(1)}, bf16[1,2,16,36,256]{4,2,3,1,0:T(8,128)(2,1)}, u32[]{:S(2)}) copy-start(bf16[1,2,16,36,256]{4,2,3,1,0:T(8,128)(2,1)} %param.7) | copy-start | bytes 1769476
  8.8 245.3 %reduce-scatter.2.cloned.1.call-start = ((), (), s32[]{:S(2)}) async-start(), calls=%async_computation.2 | async-start | bytes 3244032 | tf_op jit(solution)/shard_map/reduce_scatter | solution.py:120
  10.9 10.1 %collective-permute-start.3 = (bf16[1,1,16,36,256]{4,3,2,1,0:T(8,128)(2,1)S(1)}, bf16[1,1,16,36,256]{4,3,2,1,0:T(8,128)(2,1)S(1)}, u32[]{:S(2)}, u32[]{:S(2)}) collective-permute-start(bf16[1,1,16,36,256]{4,3,2,1,0:T(8,128)(2,1)S(1)} %get-tuple-element.25), channel_id=1, source_target_pairs={{0,1},{1,2},{2,3},{3,4},{4,5},{5,6},{6,7},{7,8},{8,9},{9,10},{10,1... | collective-permute-start | bytes 884744 | tf_op jit(solution)/shard_map/ppermute | solution.py:20
  16.4 68.7 %collective-permute-start.2 = (bf16[1,1,16,36,256]{4,3,2,1,0:T(8,128)(2,1)}, bf16[1,1,16,36,256]{4,3,2,1,0:T(8,128)(2,1)}, u32[]{:S(2)}, u32[]{:S(2)}) collective-permute-start(bf16[1,1,16,36,256]{4,3,2,1,0:T(8,128)(2,1)} %get-tuple-element.24), channel_id=1, source_target_pairs={{1,0},{2,1},{3,2},{4,3},{5,4},{6,5},{7,6},{8,7},{9,8},{10,9},{11,1... | collective-permute-start | bytes 884744 | tf_op jit(solution)/shard_map/ppermute | solution.py:23
  18.5 66.1 %copy-start.2 = (bf16[1,2,16,36,256]{4,2,3,1,0:T(8,128)(2,1)S(1)}, bf16[1,2,16,36,256]{4,2,3,1,0:T(8,128)(2,1)}, u32[]{:S(2)}) copy-start(bf16[1,2,16,36,256]{4,2,3,1,0:T(8,128)(2,1)} %param.8) | copy-start | bytes 1769476
  21.0 0.7 copy-start.12
  83.1 1.6 copy-start.1
  89.2 0.7 copy-start.15
  89.2 0.7 copy-start.16
  91.1 1.1 copy-start.5
  92.2 1.7 copy-start.3
  108.1 18.0 %collective-permute-start = (bf16[1,1,16,36,256]{4,3,2,1,0:T(8,128)(2,1)S(1)}, bf16[1,1,16,36,256]{4,3,2,1,0:T(8,128)(2,1)S(1)}, u32[]{:S(2)}, u32[]{:S(2)}) collective-permute-start(bf16[1,1,16,36,256]{4,3,2,1,0:T(8,128)(2,1)S(1)} %get-tuple-element.26), channel_id=1, source_target_pairs={{0,1},{1,2},{2,3},{3,4},{4,5},{5,6},{6,7},{7,8},{8,9},{9,10},{10,1... | collective-permute-start | bytes 884744 | tf_op jit(solution)/shard_map/ppermute | solution.py:20
  113.6 12.5 %copy-start.4 = (bf16[1,2,16,36,256]{4,2,3,1,0:T(8,128)(2,1)S(1)}, bf16[1,2,16,36,256]{4,2,3,1,0:T(8,128)(2,1)}, u32[]{:S(2)}) copy-start(bf16[1,2,16,36,256]{4,2,3,1,0:T(8,128)(2,1)} %param.8) | copy-start | bytes 1769476
  113.6 14.9 %collective-permute-start.1 = (bf16[1,1,16,36,256]{4,3,2,1,0:T(8,128)(2,1)S(1)}, bf16[1,1,16,36,256]{4,3,2,1,0:T(8,128)(2,1)S(1)}, u32[]{:S(2)}, u32[]{:S(2)}) collective-permute-start(bf16[1,1,16,36,256]{4,3,2,1,0:T(8,128)(2,1)S(1)} %get-tuple-element.27), channel_id=1, source_target_pairs={{1,0},{2,1},{3,2},{4,3},{5,4},{6,5},{7,6},{8,7},{9,8},{10,9},{11,1... | collective-permute-start | bytes 884744 | tf_op jit(solution)/shard_map/ppermute | solution.py:23
  126.1 1.2 copy-start.8
  128.5 0.7 copy-start.10
  130.4 123.6 %copy-start.6 = (bf16[1,2,16,36,256]{4,3,2,1,0:T(8,128)(2,1)S(1)}, bf16[1,2,16,36,256]{4,3,2,1,0:T(8,128)(2,1)}, u32[]{:S(2)}) copy-start(bf16[1,2,16,36,256]{4,3,2,1,0:T(8,128)(2,1)} %get-tuple-element.28) | copy-start | bytes 1769476
  130.5 232.4 %all-gather.6.cloned.1.call-start = ((), (), s32[]{:S(2)}) async-start(), calls=%async_computation.3 | async-start | bytes 1671168 | tf_op jit(solution)/shard_map/all_gather | solution.py:121
  255.0 105.3 %copy-start.11 = (bf16[1,1,16,36,256]{4,3,2,1,0:T(8,128)(2,1)S(1)}, bf16[1,1,16,36,256]{4,3,2,1,0:T(8,128)(2,1)}, u32[]{:S(2)}) copy-start(bf16[1,1,16,36,256]{4,3,2,1,0:T(8,128)(2,1)} %copy-done.10) | copy-start | bytes 884740
  360.3 1.0 copy-start.9
  361.9 2.5 copy-start.7
  361.9 2.5 copy-start.13
  361.9 2.5 copy-start.14
Sparse Core Ops, SparseCore 0:
  10.7 72.3 all-gather.3
  130.6 123.4 reduce-scatter.1
  257.2 83.4 all-gather.5
